TPU v7x, 128 devices: a whole 4x4x4 slice. The times are simulated.
128 devices in a mesh: leaf: 32 (over x, y, core), chain: 4 (over z).
Axes of the slice: x: 4, y: 4, z: 4, core: 2. Of those that a mesh axis runs over, the one named last changes fastest.
Arguments:
- right_side: float32 [32, 4096, 1024], P('leaf', 'chain'), may hold values from -6 to 6
- lower_rows: bfloat16 [32, 4096, 4096], P('leaf', 'chain'), may hold values from -0.09375 to 0.09375
- block_inverse: bfloat16 [32, 4096, 1024], P('leaf', 'chain'), may hold values from -0.1875 to 0.1875
- ancestor_cols: bfloat16 [32, 3072, 4096], P('leaf', None, 'chain'), may hold values from -0.09375 to 0.09375
- pattern: int32 [32, 24], P('leaf'), may hold values 0 or 1
- ancestor_side: float32 [3072, 1024], P('chain'), may hold values from -24 to 24
- ancestor_inverse: bfloat16 [3072, 768], P('chain'), may hold values from -0.21875 to 0.21875
Outputs:
- solution: float32 [32, 4096, 1024], P('leaf', 'chain')
- ancestor_solution: float32 [4, 768, 1024], P('chain', 'leaf')
All inputs are finite; a program needn't handle non-finite values. No bound on the sum of `pattern` on one device may be relied on, other than what follows from the above.
Results may differ from a plain program's by a relative error of at most 0.0065.
Values may be sent and summed in bfloat16 or wider, within the bound.
A program may use at most 128 MiB of HBM per device.

v0:
```python
import jax
import jax.numpy as jnp
from jax import lax
from jax.sharding import PartitionSpec as P

ROWBLK = 128


def broadcast(value, axis, root):
    mine = lax.axis_index(axis) == root
    return lax.psum(jnp.where(mine, value, jnp.zeros_like(value)), axis)


def from_partner(value, axis, stride):
    mask = 2**stride
    pairs = [(source, source ^ mask) for source in range(lax.axis_size(axis))]
    return lax.ppermute(value, axis, pairs)


def local(
    right_side, lower_rows, block_inverse, ancestor_cols, pattern, ancestor_side, ancestor_inverse
):
    rhs_rows = right_side[0]
    lower = lower_rows[0]
    inverse = block_inverse[0]
    flags = pattern[0]
    block_rows = lower.shape[0]
    chain_count = lax.axis_size("chain")
    position = lax.axis_index("chain")
    owned_rows = ancestor_side.shape[0]
    row_flags = jnp.repeat(flags.astype(jnp.float32), ROWBLK)
    pending = jnp.zeros(rhs_rows.shape, jnp.float32)
    solved = jnp.zeros(rhs_rows.shape, jnp.float32)
    arrivals = []
    for chain_step in range(chain_count):
        current = pending
        candidate = lax.cond(
            position == chain_step,
            lambda: jnp.dot(
                inverse,
                (rhs_rows - current).astype(jnp.bfloat16),
                preferred_element_type=jnp.float32,
            ),
            lambda: jnp.zeros(rhs_rows.shape, jnp.float32),
        )
        solved = solved + candidate
        arrived = broadcast(candidate.astype(jnp.bfloat16), "chain", chain_step)
        arrivals.append(arrived)
        if chain_step + 1 < chain_count:
            column_block = lower[:, chain_step * block_rows : (chain_step + 1) * block_rows]
            pending = lax.cond(
                position > chain_step,
                lambda: current
                + jnp.dot(column_block, arrived, preferred_element_type=jnp.float32),
                lambda: current,
            )
    solved_low = solved.astype(jnp.bfloat16)
    columns = ancestor_cols[0]
    product = jnp.dot(columns, solved_low, preferred_element_type=jnp.float32)
    partial_value = lax.psum_scatter(
        product * row_flags[:, None], "chain", scatter_dimension=0, tiled=True
    )
    levels = lax.axis_size("leaf").bit_length() - 1
    for level in range(levels):
        partial_value = partial_value + from_partner(partial_value, "leaf", level)
    share_rows = owned_rows // lax.axis_size("leaf")
    leaf_position = lax.axis_index("leaf")
    inverse_share = lax.dynamic_slice_in_dim(
        ancestor_inverse, leaf_position * share_rows, share_rows, 0
    )
    ancestor_solution = jnp.dot(
        inverse_share,
        (ancestor_side - partial_value).astype(jnp.bfloat16),
        preferred_element_type=jnp.float32,
    )
    return (solved[None], ancestor_solution[None])


def solution(mesh):
    return jax.shard_map(
        local,
        mesh=mesh,
        in_specs=(
            P("leaf", "chain", None),
            P("leaf", "chain", None),
            P("leaf", "chain", None),
            P("leaf", None, "chain"),
            P("leaf", None),
            P("chain", None),
            P("chain", None),
        ),
        out_specs=(P("leaf", "chain", None), P("chain", "leaf", None)),
        check_vma=False,
    )
```

profile of v0, /device:TPU:0, one launch (start us, length us, event | category | flops | bytes accessed | tf_op | source)
XLA Modules:
  0.0 701.0 jit_solution(8203343773028368888)
XLA Ops:
  7.2 7.3 %conditional.7 = (f32[1024,1024]{1,0:T(8,128)}, bf16[1024,1024]{1,0:T(8,128)(2,1)S(1)}) conditional(s32[]{:T(128)} %convert_element_type.63, () %tuple.62, (f32[1024,1024]{1,0:T(8,128)}, bf16[1024,1024]{1,0:T(8,128)(2,1)}) %tuple.117), branch_computations={%region_0.0_spmd, %region_1.0_spmd} | conditional | flops 2149580800 | bytes 12582928 | solution.py:37
  7.3 7.2 %fusion.20 = (bf16[1024,1024]{1,0:T(8,128)(2,1)S(1)}, f32[1024,1024]{1,0:T(8,128)}) fusion(bf16[1024,1024]{1,0:T(8,128)(2,1)} %get-tuple-element.59, f32[1024,1024]{1,0:T(8,128)} %get-tuple-element.60), kind=kOutput, calls=%fused_computation.30 | convolution fusion | flops 2149580800 | bytes 12582912 | tf_op jit(solution)/shard_map/cond/branch_1_fun/dot_general | solution.py:39
  16.0 58.1 %all-reduce.4.cloned.1.call-done = bf16[1024,1024]{1,0:T(8,128)(2,1)} async-done(((bf16[1024,1024]{1,0:T(8,128)(2,1)}), bf16[1024,1024]{1,0:T(8,128)(2,1)}) %all-reduce.4.cloned.1.call-update) | async-done | bytes 2097168 | tf_op jit(solution)/shard_map/psum | solution.py:11
  74.1 2.6 conditional.8
  74.1 2.5 broadcast.24
  76.6 2.8 conditional.9
  76.6 2.5 broadcast.25.clone
  79.4 1.4 broadcast_select_fusion.1
  80.9 76.0 %all-reduce.6.cloned.1.call-done = bf16[1024,1024]{1,0:T(8,128)(2,1)} async-done(((bf16[1024,1024]{1,0:T(8,128)(2,1)}), bf16[1024,1024]{1,0:T(8,128)(2,1)}) %all-reduce.6.cloned.1.call-update) | async-done | bytes 2097168 | tf_op jit(solution)/shard_map/psum | solution.py:11
  156.9 2.9 conditional.11
  156.9 2.5 broadcast.27.clone
  161.4 80.8 %all-reduce.8.cloned.1.call-done = bf16[1024,1024]{1,0:T(8,128)(2,1)} async-done(((bf16[1024,1024]{1,0:T(8,128)(2,1)}), bf16[1024,1024]{1,0:T(8,128)(2,1)}) %all-reduce.8.cloned.1.call-update) | async-done | bytes 2097168 | tf_op jit(solution)/shard_map/psum | solution.py:11
  242.3 1.6 copy-done.2
  243.8 2.5 conditional.13
  243.8 2.5 broadcast.29.clone
  246.3 7.9 %add_add_fusion = f32[1024,1024]{1,0:T(8,128)S(1)} fusion(f32[1024,1024]{1,0:T(8,128)} %get-tuple-element.98, f32[1024,1024]{1,0:T(8,128)} %get-tuple-element.96, f32[1024,1024]{1,0:T(8,128)} %get-tuple-element.86, f32[1024,1024]{1,0:T(8,128)} %get-tuple-element.94), kind=kLoop, calls=%fused_computation.18 | loop fusion | flops 3145728 | bytes 20971520 | tf_op jit(solution)/shard_map/add | solution.py:46
  254.2 2.0 copy-done.1
  256.2 12.4 %multiply_bitcast_fusion = f32[3072,1024]{0,1:T(8,128)} fusion(bf16[1,3072,1024]{2,1,0:T(8,128)(2,1)} %param.24, f32[3072]{0:T(1024)S(1)} %broadcast_bitcast_fusion, f32[1024,1024]{1,0:T(8,128)S(1)} %add_add_fusion), kind=kOutput, calls=%fused_computation.16 | convolution fusion | flops 6446645248 | bytes 23080960 | tf_op jit(solution)/shard_map/dot_general | solution.py:59
  268.6 130.9 %reduce-scatter.2.cloned.1.call-done = f32[768,1024]{0,1:T(8,128)} async-done(((f32[3072,1024]{0,1:T(8,128)}), f32[768,1024]{0,1:T(8,128)}) %reduce-scatter.2.cloned.1.call-update) | async-done | bytes 3145744 | tf_op jit(solution)/shard_map/reduce_scatter | solution.py:60
  399.5 5.9 collective-permute-done
  405.4 2.3 add.45
  407.6 1.6 collective-permute-start.1
  409.2 68.7 %collective-permute-done.1 = f32[768,1024]{0,1:T(8,128)S(1)} collective-permute-done((f32[768,1024]{0,1:T(8,128)S(1)}, f32[768,1024]{0,1:T(8,128)S(1)}, u32[]{:S(2)}, u32[]{:S(2)}) %collective-permute-start.1) | collective-permute-done | bytes 3145760 | tf_op jit(solution)/shard_map/ppermute | solution.py:17
  478.2 3.1 collective-permute-start.2
  481.3 67.8 %collective-permute-done.2 = f32[768,1024]{0,1:T(8,128)S(1)} collective-permute-done((f32[768,1024]{0,1:T(8,128)S(1)}, f32[768,1024]{0,1:T(8,128)S(1)}, u32[]{:S(2)}, u32[]{:S(2)}) %collective-permute-start.2) | collective-permute-done | bytes 3145760 | tf_op jit(solution)/shard_map/ppermute | solution.py:17
  549.5 1.5 collective-permute-start.3
  551.1 67.0 %collective-permute-done.3 = f32[768,1024]{0,1:T(8,128)S(1)} collective-permute-done((f32[768,1024]{0,1:T(8,128)S(1)}, f32[768,1024]{0,1:T(8,128)S(1)}, u32[]{:S(2)}, u32[]{:S(2)}) %collective-permute-start.3) | collective-permute-done | bytes 3145760 | tf_op jit(solution)/shard_map/ppermute | solution.py:17
  618.0 2.1 add.48
  620.1 3.0 collective-permute-start.4
  623.1 3.5 copy.14
  626.6 62.9 %collective-permute-done.4 = f32[768,1024]{0,1:T(8,128)} collective-permute-done((f32[768,1024]{0,1:T(8,128)}, f32[768,1024]{0,1:T(8,128)}, u32[]{:S(2)}, u32[]{:S(2)}) %collective-permute-start.4) | collective-permute-done | bytes 3145760 | tf_op jit(solution)/shard_map/ppermute | solution.py:17
  689.5 4.9 fusion.17
  (25 shorter events, 4.5 us)
Async XLA Ops:
  7.2 682.3 %copy-start = (bf16[768,768]{1,0:T(8,128)(2,1)S(1)}, bf16[768,768]{1,0:T(8,128)(2,1)}, u32[]{:S(2)}) copy-start(bf16[768,768]{1,0:T(8,128)(2,1)} %param.27) | copy-start | bytes 3538948
  7.2 66.9 %all-reduce.4.cloned.1.call-start = ((), (), s32[]{:S(2)}) async-start(), calls=%async_computation.1 | async-start | bytes 4194304 | tf_op jit(solution)/shard_map/psum | solution.py:11
  16.0 140.9 %all-reduce.6.cloned.1.call-start = ((), (), s32[]{:S(2)}) async-start(), calls=%async_computation.2 | async-start | bytes 4194304 | tf_op jit(solution)/shard_map/psum | solution.py:11
  80.9 161.4 %all-reduce.8.cloned.1.call-start = ((), (), s32[]{:S(2)}) async-start(), calls=%async_computation.3 | async-start | bytes 4194304 | tf_op jit(solution)/shard_map/psum | solution.py:11
  159.8 1.5 copy-start.3
  161.3 238.2 %reduce-scatter.2.cloned.1.call-start = ((), (), s32[]{:S(2)}) async-start(), calls=%async_computation.4 | async-start | bytes 15728640 | tf_op jit(solution)/shard_map/reduce_scatter | solution.py:60
  242.3 1.6 copy-start.2
  254.2 2.0 copy-start.1
  399.5 5.9 collective-permute-start
  407.6 70.2 %collective-permute-start.1 = (f32[768,1024]{0,1:T(8,128)S(1)}, f32[768,1024]{0,1:T(8,128)S(1)}, u32[]{:S(2)}, u32[]{:S(2)}) collective-permute-start(f32[768,1024]{0,1:T(8,128)S(1)} %add.45), channel_id=1, source_target_pairs={{0,8},{4,12},{8,0},{12,4},{16,24},{20,28},{24,16},{28,20},{32,40},... | collective-permute-start | bytes 9437192 | tf_op jit(solution)/shard_map/ppermute | solution.py:17
  478.2 70.9 %collective-permute-start.2 = (f32[768,1024]{0,1:T(8,128)S(1)}, f32[768,1024]{0,1:T(8,128)S(1)}, u32[]{:S(2)}, u32[]{:S(2)}) collective-permute-start(f32[768,1024]{0,1:T(8,128)S(1)} %add.46), channel_id=1, source_target_pairs={{0,16},{4,20},{8,24},{12,28},{16,0},{20,4},{24,8},{28,12},{32,48},... | collective-permute-start | bytes 9437192 | tf_op jit(solution)/shard_map/ppermute | solution.py:17
  549.5 68.5 %collective-permute-start.3 = (f32[768,1024]{0,1:T(8,128)S(1)}, f32[768,1024]{0,1:T(8,128)S(1)}, u32[]{:S(2)}, u32[]{:S(2)}) collective-permute-start(f32[768,1024]{0,1:T(8,128)S(1)} %add.47), channel_id=1, source_target_pairs={{0,32},{4,36},{8,40},{12,44},{16,48},{20,52},{24,56},{28,60},{32,0... | collective-permute-start | bytes 9437192 | tf_op jit(solution)/shard_map/ppermute | solution.py:17
  620.1 69.4 %collective-permute-start.4 = (f32[768,1024]{0,1:T(8,128)}, f32[768,1024]{0,1:T(8,128)}, u32[]{:S(2)}, u32[]{:S(2)}) collective-permute-start(f32[768,1024]{0,1:T(8,128)} %add.48), channel_id=1, source_target_pairs={{0,64},{4,68},{8,72},{12,76},{16,80},{20,84},{24,88},{28,92},{32,9... | collective-permute-start | bytes 9437192 | tf_op jit(solution)/shard_map/ppermute | solution.py:17
Sparse Core Ops, SparseCore 0:
  16.1 57.9 all-reduce.3
  81.0 75.8 all-reduce.5
  161.4 80.8 all-reduce.7
  268.7 130.7 reduce-scatter.1
where the time goes:
time: 701 us
  waiting for transfers between devices  618 us (88%)
  matrix products  24.6 us (4%)
  local copies, waits for them, and re-layouts  17.7 us (3%)
  other arithmetic  17.3 us (2%)
  between operations  13.9 us (2%)
  starting transfers between devices  9.34 us (1%)
    ppermute x5, waiting for transfers between devices, from_partner(): return lax.ppermute(value, axis, pairs)  272 us
    psum x3, waiting for transfers between devices, broadcast(): return lax.psum(jnp.where(mine, value, jnp.zeros_like(value)), axis)  215 us
    reduce_scatter x1, waiting for transfers between devices, local(): lax.psum_scatter(product * row_flags[:, None], 'chain', scatter_dimension...  131 us
  transfers between devices with their start and end apart: 9, of which 9 were waited for; matrix products, arithmetic and copies ran while one was open for 1% of the time, Pallas kernels for 0%

commit v1 on v0

v1 whole, which is shorter than its diff:
```python
import jax
import jax.numpy as jnp
from jax import lax
from jax.experimental import pallas as pl
from jax.experimental.pallas import tpu as pltpu
from jax.sharding import PartitionSpec as P

MESH = pl.DeviceIdType.MESH
ROWBLK = 128
NK = 8
W = 128
NA = 3
AHEAD = 4
B16 = jnp.bfloat16
F32 = jnp.float32


def dot(a, b):
    return jnp.dot(a, b, preferred_element_type=F32)


def wait(ref, sem):
    pltpu.make_async_copy(ref, ref, sem).wait()


def send(src, dst, ssem, rsem, leaf, chain):
    pltpu.make_async_remote_copy(
        src_ref=src,
        dst_ref=dst,
        send_sem=ssem,
        recv_sem=rsem,
        device_id=(leaf, chain),
        device_id_type=MESH,
    ).start()


def kernel(
    flags, rhs_hbm, low_hbm, inv_hbm, cols_hbm, side_hbm, ainv_hbm,
    sol_hbm, anc_hbm,
    rv, lv, iv, cv, av, sv, acc, blk, own, sx, rx, s1, r1, s2, r2, s3, r3, st, tt, ov,
    rhs_sem, in_sem, out_sem, anc_sem,
    blk_send, blk_recv, x_send, x_recv, s1_send, s1_recv, s2_send, s2_recv,
    z_send, z_recv, ag_same, ag_other, ag_recv,
):
    me = lax.axis_index("leaf")
    z = lax.axis_index("chain")
    core = lax.rem(me, 2)
    chip = lax.div(me, 2)
    x = lax.div(chip, 4)
    y = lax.rem(chip, 4)
    f = x + core * (y - x)
    g = y + core * (x - y)

    def chip_of(ff, gg):
        a, b = ff * 4 + gg, gg * 4 + ff
        return a + core * (b - a)

    chip_rows = pl.ds(pl.multiple_of(chip * 48, 48), 48)

    def rhs_load(k):
        return pltpu.make_async_copy(
            rhs_hbm.at[0, :, pl.ds(k * W, W)], rv.at[k], rhs_sem.at[k]
        )

    def low_load(j):
        return pltpu.make_async_copy(
            low_hbm.at[0, :, pl.ds(j * 1024, 1024)], lv.at[j], in_sem.at[j]
        )

    inv_load = pltpu.make_async_copy(inv_hbm.at[0], iv, in_sem.at[3])
    cols_load = pltpu.make_async_copy(cols_hbm.at[0], cv, in_sem.at[4])
    side_load = pltpu.make_async_copy(side_hbm.at[chip_rows, :], sv, in_sem.at[5])
    ainv_load = pltpu.make_async_copy(ainv_hbm.at[chip_rows, :], av, in_sem.at[6])
    inv_load.start()
    for k in range(NK):
        rhs_load(k).start()
    for j in range(3):
        @pl.when(z > j)
        def _():
            low_load(j).start()
    cols_load.start()
    side_load.start()
    ainv_load.start()

    barrier = pltpu.get_barrier_semaphore()

    @pl.loop(1, 32)
    def _(i):
        pl.semaphore_signal(
            barrier, inc=1, device_id=(lax.rem(me + i, 32), z), device_id_type=MESH
        )

    @pl.loop(1, 4)
    def _(i):
        pl.semaphore_signal(
            barrier, inc=1, device_id=(me, lax.rem(z + i, 4)), device_id_type=MESH
        )

    pl.semaphore_wait(barrier, 34)

    def send_block(j, k, slot, to):
        send(blk.at[j, k], blk.at[j, k], blk_send.at[slot, k], blk_recv.at[j, k], me, to)

    def pass_block0(k):
        wait(blk.at[0, k], blk_recv.at[0, k])
        send_block(0, k, 2, 2)

    inv_load.wait()
    for j in range(3):
        @pl.when(z > j)
        def _():
            low_load(j).wait()

    @pl.when(z == 3)
    def _():
        @pl.loop(0, AHEAD)
        def _(k):
            pass_block0(k)

    def chain(k):
        wait(rv.at[k], rhs_sem.at[k])
        acc[...] = rv[k]

        @pl.loop(0, z)
        def _(j):
            @pl.when(jnp.logical_or(z != 3, j != 0))
            def _():
                wait(blk.at[j, k], blk_recv.at[j, k])

            @pl.when(jnp.logical_and(jnp.logical_and(z == 2, j == 1), k < NA))
            def _():
                send_block(1, k, 2, 3)

            acc[...] -= dot(lv[j], blk[j, k])

        solved = dot(iv[...], acc[...].astype(B16))
        blk[z, k] = solved.astype(B16)
        rv[k] = solved

        @pl.when(z < 3)
        def _():
            send_block(z, k, 0, z + 1)

        @pl.when(jnp.logical_or(z == 0, jnp.logical_and(z == 1, k >= NA)))
        def _():
            send_block(z, k, 1, lax.rem(z + 3, 4))

        pltpu.make_async_copy(
            rv.at[k],
            sol_hbm.at[0, :, pl.ds(pl.multiple_of(k * W, W), W)],
            out_sem.at[k],
        ).start()

    def mask_columns():
        cols_load.wait()

        @pl.loop(0, 24)
        def _(i):
            rows = pl.ds(pl.multiple_of(i * ROWBLK, ROWBLK), ROWBLK)
            cv[rows, :] = cv[rows, :] * flags[0, i].astype(F32).astype(B16)

    def product(k):
        solved = blk[z, k]
        for i in range(2):
            rows = pl.ds(pl.multiple_of((1 - core) * 1536 + i * 768, 768), 768)
            sx[k, i * 768:(i + 1) * 768, :] = dot(cv[rows, :], solved).astype(B16)
        send(sx.at[k], rx.at[k], x_send.at[k], x_recv.at[k], me + 1 - 2 * core, z)
        for i in range(2):
            rows = pl.ds(pl.multiple_of(core * 1536 + i * 768, 768), 768)
            own[i * 768:(i + 1) * 768, :] = dot(cv[rows, :], solved)

    def pair_sum(k):
        wait(rx.at[k], x_recv.at[k])
        for ci in range(2):
            for ff in range(4):
                for gg in range(4):
                    rows = pl.ds(pl.multiple_of(ci * 768 + chip_of(ff, gg) * 48, 48), 48)
                    total = own[rows, :] + rx[k, rows, :].astype(F32)
                    at = ci * 192 + gg * 48
                    s1[k, ff, at:at + 48, :] = total.astype(B16)
        for d in range(1, 4):
            to = lax.rem(f + d, 4)
            send(
                s1.at[k, to], r1.at[k, d - 1], s1_send.at[k], s1_recv.at[k],
                chip_of(to, g) * 2 + core, z,
            )

    def first_sum(k):
        wait(r1.at[k], s1_recv.at[k])
        for ci in range(2):
            for gg in range(4):
                at = ci * 192 + gg * 48
                total = s1[k, f, at:at + 48, :].astype(F32)
                for d in range(3):
                    total += r1[k, d, at:at + 48, :].astype(F32)
                s2[k, gg, ci * 48:(ci + 1) * 48, :] = total.astype(B16)
        for d in range(1, 4):
            to = lax.rem(g + d, 4)
            send(
                s2.at[k, to], r2.at[k, d - 1], s2_send.at[k], s2_recv.at[k],
                chip_of(f, to) * 2 + core, z,
            )

    def second_sum(k):
        wait(r2.at[k], s2_recv.at[k])
        for ci in range(2):
            at = ci * 48
            total = s2[k, g, at:at + 48, :].astype(F32)
            for d in range(3):
                total += r2[k, d, at:at + 48, :].astype(F32)
            s3[k, ci] = total
            owner = core * 2 + ci
            away = lax.rem(owner - z + 4, 4)

            @pl.when(away != 0)
            def _():
                send(
                    s3.at[k, ci], r3.at[k, away - 1], z_send.at[k, ci], z_recv.at[k],
                    me, owner,
                )

    mine = lax.div(z, 2) == core

    def last_sum(k):
        wait(r3.at[k], z_recv.at[k])
        total = s3[k, z - 2 * core]
        for d in range(3):
            total += r3[k, d]
        here = sv[:, pl.ds(pl.multiple_of(k * W, W), W)]
        st[k] = (here - total).astype(B16)

    def share(batch, low, high):
        src = st.at[low:high]
        dst = tt.at[low:high, chip_rows, :]

        @pl.loop(0, 16)
        def _(i):
            to = lax.rem(me + 2 * i + 1, 32)
            send(src, dst, ag_other.at[batch], ag_recv.at[batch], to, z)

        @pl.loop(1, 16)
        def _(i):
            to = lax.rem(me + 2 * i, 32)
            send(src, dst, ag_same.at[batch], ag_recv.at[batch], to, z)

        pltpu.make_async_copy(src, dst, ag_recv.at[batch]).start()

    @pl.loop(0, NK)
    def _(k):
        @pl.when(jnp.logical_and(z == 3, k + AHEAD < NK))
        def _():
            pass_block0(k + AHEAD)

        chain(k)

        @pl.when(k == 0)
        def _():
            mask_columns()

        product(k)

        @pl.when(k >= 1)
        def _():
            first_sum(k - 1)

        pair_sum(k)

        @pl.when(k >= 2)
        def _():
            second_sum(k - 2)

    @pl.when(z == 0)
    def _():
        @pl.loop(NA, NK)
        def _(k):
            wait(blk.at[1, k], blk_recv.at[1, k])
            send_block(1, k, 2, 3)

    side_load.wait()
    ainv_load.wait()
    second_sum(NK - 2)

    def early():
        @pl.loop(0, NK - 1)
        def _(k):
            last_sum(k)

        share(0, 0, NK - 1)

    @pl.when(jnp.logical_and(mine, z == 3))
    def _():
        early()

    first_sum(NK - 1)
    second_sum(NK - 1)

    @pl.when(jnp.logical_and(mine, z != 3))
    def _():
        early()

    @pl.when(mine)
    def _():
        last_sum(NK - 1)
        share(1, NK - 1, NK)

    for batch, low, high in ((0, 0, NK - 1), (1, NK - 1, NK)):
        wait(tt.at[low:high], ag_recv.at[batch])
        for k in range(low, high):
            ov[:, k * W:(k + 1) * W] = dot(av[...], tt[k])
    anc_out = pltpu.make_async_copy(
        ov.at[pl.ds(pl.multiple_of(core * 24, 24), 24), :], anc_hbm.at[0], anc_sem
    )
    anc_out.start()

    @pl.loop(0, NK)
    def _(k):
        wait(rv.at[k], out_sem.at[k])

        @pl.when(z < 3)
        def _():
            wait(blk.at[0, k], blk_send.at[0, k])

        @pl.when(jnp.logical_or(z == 0, jnp.logical_and(z == 1, k >= NA)))
        def _():
            wait(blk.at[0, k], blk_send.at[1, k])

        @pl.when(jnp.logical_or(
            z == 3,
            jnp.logical_or(jnp.logical_and(z == 2, k < NA), jnp.logical_and(z == 0, k >= NA)),
        ))
        def _():
            wait(blk.at[0, k], blk_send.at[2, k])

        wait(sx.at[k], x_send.at[k])
        wait(r1.at[k], s1_send.at[k])
        wait(r2.at[k], s2_send.at[k])
        for ci in range(2):
            @pl.when(core * 2 + ci != z)
            def _():
                wait(s3.at[k, ci], z_send.at[k, ci])

    @pl.when(mine)
    def _():
        for batch, low, high in ((0, 0, NK - 1), (1, NK - 1, NK)):
            wait(tt.at[low:high], ag_other.at[batch])
            wait(tt.at[low:high, 0:720, :], ag_same.at[batch])

    anc_out.wait()


def local(
    right_side, lower_rows, block_inverse, ancestor_cols, pattern, ancestor_side, ancestor_inverse
):
    any_spec = pl.BlockSpec(memory_space=pl.ANY)
    vmem, dma = pltpu.VMEM, pltpu.SemaphoreType.DMA
    return pl.pallas_call(
        kernel,
        out_shape=(
            jax.ShapeDtypeStruct((1, 1024, 1024), F32),
            jax.ShapeDtypeStruct((1, 24, 1024), F32),
        ),
        in_specs=[pl.BlockSpec(memory_space=pltpu.SMEM)] + [any_spec] * 6,
        out_specs=(any_spec, any_spec),
        scratch_shapes=[
            vmem((NK, 1024, W), F32),
            vmem((3, 1024, 1024), B16),
            vmem((1024, 1024), B16),
            vmem((3072, 1024), B16),
            vmem((48, 768), B16),
            vmem((48, 1024), F32),
            vmem((1024, W), F32),
            vmem((4, NK, 1024, W), B16),
            vmem((1536, W), F32),
            vmem((NK, 1536, W), B16),
            vmem((NK, 1536, W), B16),
            vmem((NK, 4, 384, W), B16),
            vmem((NK, 3, 384, W), B16),
            vmem((NK, 4, 96, W), B16),
            vmem((NK, 3, 96, W), B16),
            vmem((NK, 2, 48, W), F32),
            vmem((NK, 3, 48, W), F32),
            vmem((NK, 48, W), B16),
            vmem((NK, 768, W), B16),
            vmem((48, 1024), F32),
            dma((NK,)),
            dma((7,)),
            dma((NK,)),
            dma,
            dma((3, NK)),
            dma((4, NK)),
            dma((NK,)), dma((NK,)),
            dma((NK,)), dma((NK,)),
            dma((NK,)), dma((NK,)),
            dma((NK, 2)), dma((NK,)),
            dma((2,)), dma((2,)), dma((2,)),
        ],
        compiler_params=pltpu.CompilerParams(
            collective_id=0, has_side_effects=True, vmem_limit_bytes=60 * 1024 * 1024
        ),
        name="solve",
    )(pattern, right_side, lower_rows, block_inverse, ancestor_cols, ancestor_side, ancestor_inverse)


def solution(mesh):
    return jax.shard_map(
        local,
        mesh=mesh,
        in_specs=(
            P("leaf", "chain", None),
            P("leaf", "chain", None),
            P("leaf", "chain", None),
            P("leaf", None, "chain"),
            P("leaf", None),
            P("chain", None),
            P("chain", None),
        ),
        out_specs=(P("leaf", "chain", None), P("chain", "leaf", None)),
        check_vma=False,
    )
```

time: 701 us -> 139 us (0.20)
  waiting for transfers between devices: 618 us -> 0 us
  Pallas kernels: 0 us -> 131 us
  matrix products: 24.6 us -> 0 us
  other arithmetic: 17.3 us -> 0 us
  between operations: 13.9 us -> 0.65 us
  local copies, waits for them, and re-layouts: 17.7 us -> 5.47 us
  starting transfers between devices: 9.34 us -> 0 us
    ppermute x5 -> x0, waiting for transfers between devices: 272 us -> none  [from_partner(): return lax.ppermute(value, axis, pairs)]
    psum x3 -> x0, waiting for transfers between devices: 215 us -> none  [broadcast(): return lax.psum(jnp.where(mine, value, jnp.zeros_like(value)), axis)]
    pallas_call x0 -> x1, Pallas kernels: none -> 131 us  [local(): pl.pallas_call(kernel, out_shape=(jax.ShapeDtypeStruct((1, 1024, 1024), F...]
    reduce_scatter x1 -> x0, waiting for transfers between devices: 131 us -> none  [local(): lax.psum_scatter(product * row_flags[:, None], 'chain', scatter_dimension...]
    dot_general x3 -> x0, matrix products: 24.6 us -> none  [the longest x1 12.4 us: local(): product = jnp.dot(columns, solved_low, preferred_element_type=jnp.float32)]
    add x5 -> x0, other arithmetic: 13 us -> none  [the longest x1 7.88 us: local(): solved = solved + candidate]
    another operation x6 -> x0, local copies, waits for them, and re-layouts: 10.5 us -> none
    ppermute x5 -> x0, starting transfers between devices: 9.18 us -> none  [from_partner(): return lax.ppermute(value, axis, pairs)]
  transfers between devices with their start and end apart: 9 -> 0, of which waited for: 9 -> 0; matrix products, arithmetic and copies ran while one was open for 1% -> 0% of each run, Pallas kernels for 0% -> 0%
where the time goes in v1:
time: 139 us; the launch traced here: 137 us
  Pallas kernels  131 us (94%)
  local copies, waits for them, and re-layouts  5.47 us (4%)
    pallas_call x1, Pallas kernels, local(): pl.pallas_call(kernel, out_shape=(jax.ShapeDtypeStruct((1, 1024, 1024), F...  131 us
    unnamed x4, local copies, waits for them, and re-layouts  5.47 us

profile of v1, /device:TPU:0, one launch (start us, length us, event | category | flops | bytes accessed | tf_op | source)
XLA Modules:
  0.0 137.0 jit_solution(2226792520001318366)
XLA Ops:
  0.6 130.9 %solve.1 = (f32[1,1024,1024]{2,1,0:T(8,128)}, f32[1,24,1024]{2,1,0:T(8,128)}) custom-call(s32[1,24]{1,0:T(1,128)} %flags.1, f32[1,1024,1024]{2,1,0:T(8,128)} %rhs_hbm.1, bf16[1,1024,4096]{2,1,0:T(8,128)(2,1)} %low_hbm.1, bf16[1,1024,1024]{2,1,0:T(8,128)(2,1)} %inv_hbm.1, bf16[1,3072,1024]{2,1,0:T(8,128)(2,1)} %cols_hbm.1, f32[768,1024]{1,0:T(8,128)} %side_hbm.1, ...), custom_call_target="tpu_custom_call" | custom-call | tf_op jit(solution)/shard_map/solve/pallas_call | solution.py:356
  131.5 0.0 copy-start
  131.5 4.8 %copy.11 = f32[1,1024,1024]{2,1,0:T(8,128)} copy(f32[1,1024,1024]{2,1,0:T(8,128)} %get-tuple-element.4) | data formatting | bytes 8388608
  136.4 0.0 copy-done
  136.4 0.6 copy.12
Async XLA Ops:
  131.5 4.8 %copy-start = (f32[1,24,1024]{2,1,0:T(8,128)S(1)}, f32[1,24,1024]{2,1,0:T(8,128)}, u32[]{:S(2)}) copy-start(f32[1,24,1024]{2,1,0:T(8,128)} %get-tuple-element.5) | copy-start | bytes 294916

commit v2 on v1

v2 whole, which is shorter than its diff:
```python
import jax
import jax.numpy as jnp
from jax import lax
from jax.experimental import pallas as pl
from jax.experimental.pallas import tpu as pltpu
from jax.sharding import PartitionSpec as P

MESH = pl.DeviceIdType.MESH
ROWBLK = 128
NK = 8
W = 128
NA = 3
AHEAD = 5
B16 = jnp.bfloat16
F32 = jnp.float32


def dot(a, b):
    return jnp.dot(a, b, preferred_element_type=F32)


def wait(ref, sem):
    pltpu.make_async_copy(ref, ref, sem).wait()


def send(src, dst, ssem, rsem, leaf, chain):
    pltpu.make_async_remote_copy(
        src_ref=src,
        dst_ref=dst,
        send_sem=ssem,
        recv_sem=rsem,
        device_id=(leaf, chain),
        device_id_type=MESH,
    ).start()


def kernel(
    flags, rhs_hbm, low_hbm, inv_hbm, cols_hbm, side_hbm, ainv_hbm,
    sol, anc,
    lv, iv, cv, av, sv, blk, own, sx, rx, s1, r1, s2, r2, s3, r3, st, tf, ov,
    rhs_sem, in_sem,
    blk_send, blk_recv, x_send, x_recv, s1_send, s1_recv, s2_send, s2_recv,
    z_send, z_recv, ag_send, ag_recv, o_send, o_recv,
):
    me = lax.axis_index("leaf")
    z = lax.axis_index("chain")
    core = lax.rem(me, 2)
    chip = lax.div(me, 2)
    x = lax.div(chip, 4)
    y = lax.rem(chip, 4)
    f = x + core * (y - x)
    g = y + core * (x - y)

    def chip_of(ff, gg):
        a, b = ff * 4 + gg, gg * 4 + ff
        return a + core * (b - a)

    chip_rows = pl.ds(pl.multiple_of(chip * 48, 48), 48)

    def columns_of(k):
        return pl.ds(k * W if isinstance(k, int) else pl.multiple_of(k * W, W), W)

    def rhs_load(k):
        return pltpu.make_async_copy(
            rhs_hbm.at[0, :, columns_of(k)], sol.at[0, :, columns_of(k)], rhs_sem.at[k]
        )

    def low_load(j):
        return pltpu.make_async_copy(
            low_hbm.at[0, :, pl.ds(j * 1024, 1024)], lv.at[j], in_sem.at[j]
        )

    inv_load = pltpu.make_async_copy(inv_hbm.at[0], iv, in_sem.at[3])
    def cols_load(half):
        here = pl.ds(pl.multiple_of((half + (1 - 2 * half) * (1 - core)) * 1536, 1536), 1536)
        return pltpu.make_async_copy(
            cols_hbm.at[0, here, :], cv.at[half * 1536:(half + 1) * 1536], in_sem.at[4 + half]
        )

    side_load = pltpu.make_async_copy(side_hbm.at[chip_rows, :], sv, in_sem.at[6])
    ainv_load = pltpu.make_async_copy(ainv_hbm.at[chip_rows, :], av, in_sem.at[7])
    inv_load.start()
    rhs_load(0).start()

    barrier = pltpu.get_barrier_semaphore()

    def greet(leaf, chain):
        pl.semaphore_signal(barrier, inc=1, device_id=(leaf, chain), device_id_type=MESH)

    partner = me + 1 - 2 * core
    greet(partner, z)
    for d in range(1, 4):
        greet(me, lax.rem(z + d, 4))

    @pl.loop(1, 16)
    def _(i):
        greet(lax.rem(me + 2 * i, 32), z)

    def solve(k):
        solved = dot(iv[...], sol[0, :, columns_of(k)].astype(B16))
        blk[z, k] = solved.astype(B16)
        sol[0, :, columns_of(k)] = solved

    def send_block(j, k, slot, to):
        send(blk.at[j, k], blk.at[j, k], blk_send.at[slot, k], blk_recv.at[j, k], me, to)

    def send_solved(k):
        @pl.when(z < 3)
        def _():
            send_block(z, k, 0, z + 1)

        @pl.when(jnp.logical_or(z == 0, jnp.logical_and(z == 1, k >= NA)))
        def _():
            send_block(z, k, 1, lax.rem(z + 3, 4))

    def pass_block0(k):
        wait(blk.at[0, k], blk_recv.at[0, k])
        send_block(0, k, 2, 2)
        sol[0, :, columns_of(k)] -= dot(lv[0], blk[0, k])

    inv_load.wait()
    rhs_load(0).wait()
    for k in range(1, NK):
        rhs_load(k).start()
    for j in range(3):
        @pl.when(z > j)
        def _():
            low_load(j).start()
    cols_load(0).start()
    cols_load(1).start()
    side_load.start()
    ainv_load.start()

    @pl.when(z == 0)
    def _():
        solve(0)

    pl.semaphore_wait(barrier, 19)

    @pl.when(z == 0)
    def _():
        send_solved(0)

    for k in range(1, NK):
        rhs_load(k).wait()

    for j in range(3):
        @pl.when(z > j)
        def _():
            low_load(j).wait()

    @pl.when(z == 3)
    def _():
        @pl.loop(0, AHEAD)
        def _(k):
            pass_block0(k)

    def chain(k):
        @pl.loop(lax.div(z, 3), z)
        def _(j):
            wait(blk.at[j, k], blk_recv.at[j, k])

            @pl.when(jnp.logical_and(jnp.logical_and(z == 2, j == 1), k < NA))
            def _():
                send_block(1, k, 2, 3)

            sol[0, :, columns_of(k)] -= dot(lv[j], blk[j, k])

        @pl.when(z + k > 0)
        def _():
            solve(k)
            send_solved(k)

    def mask_columns():
        for half in range(2):
            cols_load(half).wait()

        @pl.loop(0, 24)
        def _(i):
            rows = pl.ds(pl.multiple_of(i * ROWBLK, ROWBLK), ROWBLK)
            entry = lax.rem(i + 12 * (1 - core), 24)
            cv[rows, :] = cv[rows, :] * flags[0, entry].astype(F32).astype(B16)

    def product(chunks):
        solved = jnp.concatenate([blk[z, k] for k in chunks], axis=1)
        part = dot(cv[0:1536, :], solved)
        for i, k in enumerate(chunks):
            sx[k] = part[:, i * W:(i + 1) * W].astype(B16)
            send(sx.at[k], rx.at[k], x_send.at[k], x_recv.at[k], partner, z)
        part = dot(cv[1536:3072, :], solved)
        for i in range(len(chunks)):
            own[i] = part[:, i * W:(i + 1) * W]

    def pair_sum(k, slot):
        wait(rx.at[k], x_recv.at[k])
        for ff in range(4):
            for ci in range(2):
                for gg in range(4):
                    rows = pl.ds(pl.multiple_of(ci * 768 + chip_of(ff, gg) * 48, 48), 48)
                    total = own[slot, rows, :] + rx[k, rows, :].astype(F32)
                    at = ci * 192 + gg * 48
                    s1[k, ff, at:at + 48, :] = total.astype(B16)
        for d in range(1, 4):
            to = lax.rem(f + d, 4)
            send(
                s1.at[k, to], r1.at[k, d - 1], s1_send.at[k], s1_recv.at[k],
                chip_of(to, g) * 2 + core, z,
            )

    def first_sum(k):
        wait(r1.at[k], s1_recv.at[k])
        for ci in range(2):
            for gg in range(4):
                at = ci * 192 + gg * 48
                total = s1[k, f, at:at + 48, :].astype(F32)
                for d in range(3):
                    total += r1[k, d, at:at + 48, :].astype(F32)
                s2[k, gg, ci * 48:(ci + 1) * 48, :] = total.astype(B16)
        for d in range(1, 4):
            to = lax.rem(g + d, 4)
            send(
                s2.at[k, to], r2.at[k, d - 1], s2_send.at[k], s2_recv.at[k],
                chip_of(f, to) * 2 + core, z,
            )

    def second_sum(k):
        wait(r2.at[k], s2_recv.at[k])
        for ci in range(2):
            at = ci * 48
            total = s2[k, g, at:at + 48, :].astype(F32)
            for d in range(3):
                total += r2[k, d, at:at + 48, :].astype(F32)
            s3[k, ci] = total
            owner = core * 2 + ci
            away = lax.rem(owner - z + 4, 4)

            @pl.when(away != 0)
            def _():
                send(
                    s3.at[k, ci], r3.at[k, away - 1], z_send.at[k, ci], z_recv.at[k],
                    me, owner,
                )

    mine = lax.div(z, 2) == core

    def last_sum(k):
        wait(r3.at[k], z_recv.at[k])
        total = s3[k, z - 2 * core]
        for d in range(3):
            total += r3[k, d]
        here = sv[:, pl.ds(pl.multiple_of(k * W, W), W)]
        st[k] = (here - total).astype(B16)

        @pl.loop(1, 16)
        def _(i):
            to = lax.rem(me + 2 * i, 32)
            send(st.at[k], tf.at[k, chip], ag_send.at[k], ag_recv.at[k], to, z)

        tf[k, chip] = st[k]

    def finish(k):
        wait(tf.at[k, 0:15], ag_recv.at[k])
        result = dot(av[...], jnp.concatenate([tf[k, i] for i in range(16)], axis=0))
        ov[k, 0] = result[:24]
        ov[k, 1] = result[24:]
        send(
            ov.at[k, 1 - core], anc.at[0, :, columns_of(k)], o_send.at[k], o_recv.at[k],
            partner, z,
        )
        anc[0, :, columns_of(k)] = ov[k, core]

    def last_plane(step, chunks):
        @pl.when(jnp.logical_and(mine, z == 3))
        def _():
            for k in chunks:
                step(k)

    @pl.loop(0, 3)
    def _(m):
        for i in range(2):
            k = m * 2 + i

            chain(k)

            @pl.when(jnp.logical_and(z == 3, k + AHEAD < NK))
            def _():
                pass_block0(k + AHEAD)

        @pl.when(m == 0)
        def _():
            mask_columns()
            side_load.wait()
            ainv_load.wait()

        product((m * 2, m * 2 + 1))

        @pl.when(m >= 1)
        def _():
            for i in range(2):
                first_sum(m * 2 - 2 + i)

        for i in range(2):
            pair_sum(m * 2 + i, i)

        @pl.when(m >= 2)
        def _():
            for i in range(2):
                second_sum(m * 2 - 4 + i)

            last_plane(last_sum, (0, 1))

    chain(6)
    product((6,))
    second_sum(2)
    second_sum(3)
    pair_sum(6, 0)
    last_plane(last_sum, (2, 3))
    chain(7)
    product((7,))
    first_sum(4)
    first_sum(5)
    pair_sum(7, 0)

    @pl.when(z == 0)
    def _():
        @pl.loop(NA, NK)
        def _(k):
            wait(blk.at[1, k], blk_recv.at[1, k])
            send_block(1, k, 2, 3)

    first_sum(6)
    second_sum(4)
    second_sum(5)
    first_sum(7)
    last_plane(last_sum, (4, 5))
    second_sum(6)
    last_plane(last_sum, (6,))
    second_sum(7)

    @pl.when(jnp.logical_and(mine, z != 3))
    def _():
        @pl.loop(0, NK - 1)
        def _(k):
            last_sum(k)

            @pl.when(k >= 1)
            def _():
                finish(k - 1)

    @pl.when(mine)
    def _():
        last_sum(7)

    last_plane(finish, range(0, 6))

    @pl.when(mine)
    def _():
        finish(6)
        finish(7)

    @pl.loop(0, NK)
    def _(k):
        @pl.when(z < 3)
        def _():
            wait(blk.at[0, k], blk_send.at[0, k])

        @pl.when(jnp.logical_or(z == 0, jnp.logical_and(z == 1, k >= NA)))
        def _():
            wait(blk.at[0, k], blk_send.at[1, k])

        @pl.when(jnp.logical_or(
            z == 3,
            jnp.logical_or(jnp.logical_and(z == 2, k < NA), jnp.logical_and(z == 0, k >= NA)),
        ))
        def _():
            wait(blk.at[0, k], blk_send.at[2, k])

        wait(sx.at[k], x_send.at[k])
        wait(r1.at[k], s1_send.at[k])
        wait(r2.at[k], s2_send.at[k])
        for ci in range(2):
            @pl.when(core * 2 + ci != z)
            def _():
                wait(s3.at[k, ci], z_send.at[k, ci])

        @pl.when(mine)
        def _():
            wait(tf.at[k, 0:15], ag_send.at[k])
            wait(ov.at[k, 0], o_send.at[k])

        @pl.when(jnp.logical_not(mine))
        def _():
            wait(ov.at[k, 0], o_recv.at[k])


def local(
    right_side, lower_rows, block_inverse, ancestor_cols, pattern, ancestor_side, ancestor_inverse
):
    any_spec = pl.BlockSpec(memory_space=pl.ANY)
    vmem, dma = pltpu.VMEM, pltpu.SemaphoreType.DMA
    return pl.pallas_call(
        kernel,
        out_shape=(
            pltpu.VMEM((1, 1024, 1024), F32),
            pltpu.VMEM((1, 24, 1024), F32),
        ),
        in_specs=[pl.BlockSpec(memory_space=pltpu.SMEM)] + [any_spec] * 6,
        out_specs=(pl.BlockSpec(memory_space=vmem),) * 2,
        scratch_shapes=[
            vmem((3, 1024, 1024), B16),
            vmem((1024, 1024), B16),
            vmem((3072, 1024), B16),
            vmem((48, 768), B16),
            vmem((48, 1024), F32),
            vmem((4, NK, 1024, W), B16),
            vmem((2, 1536, W), F32),
            vmem((NK, 1536, W), B16),
            vmem((NK, 1536, W), B16),
            vmem((NK, 4, 384, W), B16),
            vmem((NK, 3, 384, W), B16),
            vmem((NK, 4, 96, W), B16),
            vmem((NK, 3, 96, W), B16),
            vmem((NK, 2, 48, W), F32),
            vmem((NK, 3, 48, W), F32),
            vmem((NK, 48, W), B16),
            vmem((NK, 16, 48, W), B16),
            vmem((NK, 2, 24, W), F32),
            dma((NK,)),
            dma((8,)),
            dma((3, NK)),
            dma((4, NK)),
            dma((NK,)), dma((NK,)),
            dma((NK,)), dma((NK,)),
            dma((NK,)), dma((NK,)),
            dma((NK, 2)), dma((NK,)),
            dma((NK,)), dma((NK,)),
            dma((NK,)), dma((NK,)),
        ],
        compiler_params=pltpu.CompilerParams(
            collective_id=0, has_side_effects=True, vmem_limit_bytes=52 * 1024 * 1024
        ),
        name="solve",
    )(pattern, right_side, lower_rows, block_inverse, ancestor_cols, ancestor_side, ancestor_inverse)


def solution(mesh):
    return jax.shard_map(
        local,
        mesh=mesh,
        in_specs=(
            P("leaf", "chain", None),
            P("leaf", "chain", None),
            P("leaf", "chain", None),
            P("leaf", None, "chain"),
            P("leaf", None),
            P("chain", None),
            P("chain", None),
        ),
        out_specs=(P("leaf", "chain", None), P("chain", "leaf", None)),
        check_vma=False,
    )
```

time: 139 us -> 121 us (0.87)
  Pallas kernels: 131 us -> 116 us
  local copies, waits for them, and re-layouts: 5.47 us -> 2.66 us
    pallas_call x1, Pallas kernels: 131 us -> 116 us  [local(): pl.pallas_call(kernel, out_shape=(pltpu.VMEM((1, 1024, 1024), F32), pltpu...]
    unnamed x4 -> x2, local copies, waits for them, and re-layouts: 5.47 us -> 2.66 us
where the time goes in v2:
time: 121 us; the launch traced here: 119 us
  Pallas kernels  116 us (96%)
  local copies, waits for them, and re-layouts  2.66 us (2%)
    pallas_call x1, Pallas kernels, local(): pl.pallas_call(kernel, out_shape=(pltpu.VMEM((1, 1024, 1024), F32), pltpu...  116 us
    unnamed x2, local copies, waits for them, and re-layouts  2.66 us

profile of v2, /device:TPU:0, one launch (start us, length us, event | category | flops | bytes accessed | tf_op | source)
XLA Modules:
  0.0 119.5 jit_solution(16178985719301360496)
XLA Ops:
  0.6 116.2 %solve.1 = (f32[1,1024,1024]{2,1,0:T(8,128)S(1)}, f32[1,24,1024]{2,1,0:T(8,128)S(1)}) custom-call(s32[1,24]{1,0:T(1,128)} %flags.1, f32[1,1024,1024]{2,1,0:T(8,128)} %rhs_hbm.1, bf16[1,1024,4096]{2,1,0:T(8,128)(2,1)} %low_hbm.1, bf16[1,1024,1024]{2,1,0:T(8,128)(2,1)} %inv_hbm.1, bf16[1,3072,1024]{2,1,0:T(8,128)(2,1)} %cols_hbm.1, f32[768,1024]{1,0:T(8,128)} %side_hbm.1, ...), custom_call_target="tpu_custom_call" | custom-call | tf_op jit(solution)/shard_map/solve/pallas_call | solution.py:401
  116.8 2.0 %copy.11 = f32[1,1024,1024]{2,1,0:T(8,128)} copy(f32[1,1024,1024]{2,1,0:T(8,128)S(1)} %get-tuple-element.2) | data formatting | bytes 8388608
  118.9 0.6 copy.12

commit v3 on v2

--- a/solution.py
+++ b/solution.py
@@ -37,10 +37,10 @@
 def kernel(
     flags, rhs_hbm, low_hbm, inv_hbm, cols_hbm, side_hbm, ainv_hbm,
     sol, anc,
-    lv, iv, cv, av, sv, blk, own, sx, rx, s1, r1, s2, r2, s3, r3, st, tf, ov,
+    lv, iv, cv, av, sv, blk, own, sx, rx, s1, r1, s2, r2, s3, r3, rw, st, tf, ov,
     rhs_sem, in_sem,
     blk_send, blk_recv, x_send, x_recv, s1_send, s1_recv, s2_send, s2_recv,
-    z_send, z_recv, ag_send, ag_recv, o_send, o_recv,
+    z_send, z_recv, w_send, w_recv, ag_send, ag_recv, o_send, o_recv,
 ):
     me = lax.axis_index("leaf")
     z = lax.axis_index("chain")
@@ -91,10 +91,8 @@
     greet(partner, z)
     for d in range(1, 4):
         greet(me, lax.rem(z + d, 4))
-
-    @pl.loop(1, 16)
-    def _(i):
-        greet(lax.rem(me + 2 * i, 32), z)
+        greet(chip_of(lax.rem(f + d, 4), g) * 2 + core, z)
+        greet(chip_of(f, lax.rem(g + d, 4)) * 2 + core, z)
 
     def solve(k):
         solved = dot(iv[...], sol[0, :, columns_of(k)].astype(B16))
@@ -135,7 +133,7 @@
     def _():
         solve(0)
 
-    pl.semaphore_wait(barrier, 19)
+    pl.semaphore_wait(barrier, 10)
 
     @pl.when(z == 0)
     def _():
@@ -186,10 +184,11 @@
         part = dot(cv[0:1536, :], solved)
         for i, k in enumerate(chunks):
             sx[k] = part[:, i * W:(i + 1) * W].astype(B16)
-            send(sx.at[k], rx.at[k], x_send.at[k], x_recv.at[k], partner, z)
         part = dot(cv[1536:3072, :], solved)
         for i in range(len(chunks)):
             own[i] = part[:, i * W:(i + 1) * W]
+        for k in chunks:
+            send(sx.at[k], rx.at[k], x_send.at[k], x_recv.at[k], partner, z)
 
     def pair_sum(k, slot):
         wait(rx.at[k], x_recv.at[k])
@@ -207,7 +206,7 @@
                 chip_of(to, g) * 2 + core, z,
             )
 
-    def first_sum(k):
+    def first_total(k):
         wait(r1.at[k], s1_recv.at[k])
         for ci in range(2):
             for gg in range(4):
@@ -216,12 +215,36 @@
                 for d in range(3):
                     total += r1[k, d, at:at + 48, :].astype(F32)
                 s2[k, gg, ci * 48:(ci + 1) * 48, :] = total.astype(B16)
+
+    def first_sum(k):
+        first_total(k)
         for d in range(1, 4):
             to = lax.rem(g + d, 4)
             send(
                 s2.at[k, to], r2.at[k, d - 1], s2_send.at[k], s2_recv.at[k],
                 chip_of(f, to) * 2 + core, z,
             )
+
+    def wide_send(k):
+        first_total(k)
+        slot = z * 4 + g
+        for ci in range(2):
+            owner = core * 2 + ci
+            for d in range(4):
+                to = lax.rem(g + d, 4)
+                piece = s2.at[k, to, ci * 48:(ci + 1) * 48, :]
+
+                def go():
+                    send(piece, rw.at[slot], w_send, w_recv, chip_of(f, to) * 2 + core, owner)
+
+                if d > 0:
+                    go()
+                else:
+                    pl.when(owner != z)(go)
+
+                    @pl.when(owner == z)
+                    def _():
+                        rw[slot] = piece[...]
 
     def second_sum(k):
         wait(r2.at[k], s2_recv.at[k])
@@ -243,11 +266,21 @@
 
     mine = lax.div(z, 2) == core
 
+    def wide_sum(k):
+        wait(rw.at[0:15], w_recv)
+        total = rw[0].astype(F32)
+        for i in range(1, 16):
+            total += rw[i].astype(F32)
+        gather(k, total)
+
     def last_sum(k):
         wait(r3.at[k], z_recv.at[k])
         total = s3[k, z - 2 * core]
         for d in range(3):
             total += r3[k, d]
+        gather(k, total)
+
+    def gather(k, total):
         here = sv[:, pl.ds(pl.multiple_of(k * W, W), W)]
         st[k] = (here - total).astype(B16)
 
@@ -307,19 +340,18 @@
             for i in range(2):
                 second_sum(m * 2 - 4 + i)
 
-            last_plane(last_sum, (0, 1))
-
     chain(6)
     product((6,))
     second_sum(2)
     second_sum(3)
+    chain(7)
     pair_sum(6, 0)
-    last_plane(last_sum, (2, 3))
-    chain(7)
     product((7,))
     first_sum(4)
     first_sum(5)
     pair_sum(7, 0)
+    second_sum(4)
+    second_sum(5)
 
     @pl.when(z == 0)
     def _():
@@ -329,13 +361,9 @@
             send_block(1, k, 2, 3)
 
     first_sum(6)
-    second_sum(4)
-    second_sum(5)
-    first_sum(7)
-    last_plane(last_sum, (4, 5))
+    wide_send(7)
     second_sum(6)
-    last_plane(last_sum, (6,))
-    second_sum(7)
+    last_plane(last_sum, range(0, 7))
 
     @pl.when(jnp.logical_and(mine, z != 3))
     def _():
@@ -343,20 +371,21 @@
         def _(k):
             last_sum(k)
 
-            @pl.when(k >= 1)
-            def _():
-                finish(k - 1)
-
     @pl.when(mine)
     def _():
-        last_sum(7)
-
-    last_plane(finish, range(0, 6))
+        wide_sum(7)
+
+        @pl.loop(0, NK)
+        def _(k):
+            finish(k)
 
     @pl.when(mine)
     def _():
-        finish(6)
-        finish(7)
+        wait(rw.at[0:7], w_send)
+
+    @pl.when(jnp.logical_not(mine))
+    def _():
+        wait(rw.at[0:8], w_send)
 
     @pl.loop(0, NK)
     def _(k):
@@ -377,11 +406,14 @@
 
         wait(sx.at[k], x_send.at[k])
         wait(r1.at[k], s1_send.at[k])
-        wait(r2.at[k], s2_send.at[k])
-        for ci in range(2):
-            @pl.when(core * 2 + ci != z)
-            def _():
-                wait(s3.at[k, ci], z_send.at[k, ci])
+
+        @pl.when(k < NK - 1)
+        def _():
+            wait(r2.at[k], s2_send.at[k])
+            for ci in range(2):
+                @pl.when(core * 2 + ci != z)
+                def _():
+                    wait(s3.at[k, ci], z_send.at[k, ci])
 
         @pl.when(mine)
         def _():
@@ -422,6 +454,7 @@
             vmem((NK, 3, 96, W), B16),
             vmem((NK, 2, 48, W), F32),
             vmem((NK, 3, 48, W), F32),
+            vmem((16, 48, W), B16),
             vmem((NK, 48, W), B16),
             vmem((NK, 16, 48, W), B16),
             vmem((NK, 2, 24, W), F32),
@@ -433,6 +466,7 @@
             dma((NK,)), dma((NK,)),
             dma((NK,)), dma((NK,)),
             dma((NK, 2)), dma((NK,)),
+            dma, dma,
             dma((NK,)), dma((NK,)),
             dma((NK,)), dma((NK,)),
         ],

time: 121 us -> 116 us (0.959)
  Pallas kernels: 116 us -> 111 us
    pallas_call x1, Pallas kernels: 116 us -> 111 us  [local(): pl.pallas_call(kernel, out_shape=(pltpu.VMEM((1, 1024, 1024), F32), pltpu...]
where the time goes in v3:
time: 116 us; the launch traced here: 115 us
  Pallas kernels  111 us (96%)
  local copies, waits for them, and re-layouts  2.66 us (2%)
    pallas_call x1, Pallas kernels, local(): pl.pallas_call(kernel, out_shape=(pltpu.VMEM((1, 1024, 1024), F32), pltpu...  111 us
    unnamed x2, local copies, waits for them, and re-layouts  2.66 us

profile of v3, /device:TPU:0, one launch (start us, length us, event | category | flops | bytes accessed | tf_op | source)
XLA Modules:
  0.0 114.5 jit_solution(14670345109518367562)
XLA Ops:
  0.6 111.3 %solve.1 = (f32[1,1024,1024]{2,1,0:T(8,128)S(1)}, f32[1,24,1024]{2,1,0:T(8,128)S(1)}) custom-call(s32[1,24]{1,0:T(1,128)} %flags.1, f32[1,1024,1024]{2,1,0:T(8,128)} %rhs_hbm.1, bf16[1,1024,4096]{2,1,0:T(8,128)(2,1)} %low_hbm.1, bf16[1,1024,1024]{2,1,0:T(8,128)(2,1)} %inv_hbm.1, bf16[1,3072,1024]{2,1,0:T(8,128)(2,1)} %cols_hbm.1, f32[768,1024]{1,0:T(8,128)} %side_hbm.1, ...), custom_call_target="tpu_custom_call" | custom-call | tf_op jit(solution)/shard_map/solve/pallas_call | solution.py:433
  111.9 2.0 %copy.11 = f32[1,1024,1024]{2,1,0:T(8,128)} copy(f32[1,1024,1024]{2,1,0:T(8,128)S(1)} %get-tuple-element.2) | data formatting | bytes 8388608
  113.9 0.6 copy.12

commit v4 on v3

--- a/solution.py
+++ b/solution.py
@@ -62,7 +62,7 @@
 
     def rhs_load(k):
         return pltpu.make_async_copy(
-            rhs_hbm.at[0, :, columns_of(k)], sol.at[0, :, columns_of(k)], rhs_sem.at[k]
+            rhs_hbm.at[0, :, columns_of(k)], sol.at[0, :, columns_of(k)], rhs_sem.at[min(k, 1)]
         )
 
     def low_load(j):
@@ -100,7 +100,7 @@
         sol[0, :, columns_of(k)] = solved
 
     def send_block(j, k, slot, to):
-        send(blk.at[j, k], blk.at[j, k], blk_send.at[slot, k], blk_recv.at[j, k], me, to)
+        send(blk.at[j, k], blk.at[j, k], blk_send.at[slot], blk_recv.at[j, k], me, to)
 
     def send_solved(k):
         @pl.when(z < 3)
@@ -139,8 +139,7 @@
     def _():
         send_solved(0)
 
-    for k in range(1, NK):
-        rhs_load(k).wait()
+    wait(sol.at[0, :, W:NK * W], rhs_sem.at[1])
 
     for j in range(3):
         @pl.when(z > j)
@@ -188,7 +187,7 @@
         for i in range(len(chunks)):
             own[i] = part[:, i * W:(i + 1) * W]
         for k in chunks:
-            send(sx.at[k], rx.at[k], x_send.at[k], x_recv.at[k], partner, z)
+            send(sx.at[k], rx.at[k], x_send, x_recv.at[k], partner, z)
 
     def pair_sum(k, slot):
         wait(rx.at[k], x_recv.at[k])
@@ -202,7 +201,7 @@
         for d in range(1, 4):
             to = lax.rem(f + d, 4)
             send(
-                s1.at[k, to], r1.at[k, d - 1], s1_send.at[k], s1_recv.at[k],
+                s1.at[k, to], r1.at[k, d - 1], s1_send, s1_recv.at[k],
                 chip_of(to, g) * 2 + core, z,
             )
 
@@ -221,7 +220,7 @@
         for d in range(1, 4):
             to = lax.rem(g + d, 4)
             send(
-                s2.at[k, to], r2.at[k, d - 1], s2_send.at[k], s2_recv.at[k],
+                s2.at[k, to], r2.at[k, d - 1], s2_send, s2_recv.at[k],
                 chip_of(f, to) * 2 + core, z,
             )
 
@@ -260,7 +259,7 @@
             @pl.when(away != 0)
             def _():
                 send(
-                    s3.at[k, ci], r3.at[k, away - 1], z_send.at[k, ci], z_recv.at[k],
+                    s3.at[k, ci], r3.at[k, away - 1], z_send, z_recv.at[k],
                     me, owner,
                 )
 
@@ -287,7 +286,7 @@
         @pl.loop(1, 16)
         def _(i):
             to = lax.rem(me + 2 * i, 32)
-            send(st.at[k], tf.at[k, chip], ag_send.at[k], ag_recv.at[k], to, z)
+            send(st.at[k], tf.at[k, chip], ag_send, ag_recv.at[k], to, z)
 
         tf[k, chip] = st[k]
 
@@ -297,7 +296,7 @@
         ov[k, 0] = result[:24]
         ov[k, 1] = result[24:]
         send(
-            ov.at[k, 1 - core], anc.at[0, :, columns_of(k)], o_send.at[k], o_recv.at[k],
+            ov.at[k, 1 - core], anc.at[0, :, columns_of(k)], o_send, o_recv,
             partner, z,
         )
         anc[0, :, columns_of(k)] = ov[k, core]
@@ -339,6 +338,7 @@
         def _():
             for i in range(2):
                 second_sum(m * 2 - 4 + i)
+            last_plane(last_sum, (0,))
 
     chain(6)
     product((6,))
@@ -350,8 +350,6 @@
     first_sum(4)
     first_sum(5)
     pair_sum(7, 0)
-    second_sum(4)
-    second_sum(5)
 
     @pl.when(z == 0)
     def _():
@@ -361,9 +359,10 @@
             send_block(1, k, 2, 3)
 
     first_sum(6)
+    second_sum(4)
+    second_sum(5)
     wide_send(7)
     second_sum(6)
-    last_plane(last_sum, range(0, 7))
 
     @pl.when(jnp.logical_and(mine, z != 3))
     def _():
@@ -375,54 +374,50 @@
     def _():
         wide_sum(7)
 
+    last_plane(last_sum, range(1, 7))
+
+    @pl.when(z < 3)
+    def _():
+        wait(blk.at[0], blk_send.at[0])
+
+    @pl.when(z == 0)
+    def _():
+        wait(blk.at[0], blk_send.at[1])
+        wait(blk.at[0, NA:NK], blk_send.at[2])
+
+    @pl.when(z == 1)
+    def _():
+        wait(blk.at[0, NA:NK], blk_send.at[1])
+
+    @pl.when(z == 2)
+    def _():
+        wait(blk.at[0, 0:NA], blk_send.at[2])
+
+    @pl.when(z == 3)
+    def _():
+        wait(blk.at[0], blk_send.at[2])
+
+    wait(sx, x_send)
+    wait(r1, s1_send)
+    wait(r2.at[0:NK - 1], s2_send)
+
+    @pl.when(mine)
+    def _():
+        wait(s3.at[0:NK - 1, 0], z_send)
+        wait(rw.at[0:7], w_send)
+
         @pl.loop(0, NK)
         def _(k):
             finish(k)
 
-    @pl.when(mine)
-    def _():
-        wait(rw.at[0:7], w_send)
+        wait(tf.at[:, 0:15], ag_send)
+        wait(ov.at[:, 0], o_send)
 
     @pl.when(jnp.logical_not(mine))
     def _():
+        wait(s3.at[0:NK - 1], z_send)
         wait(rw.at[0:8], w_send)
-
-    @pl.loop(0, NK)
-    def _(k):
-        @pl.when(z < 3)
-        def _():
-            wait(blk.at[0, k], blk_send.at[0, k])
-
-        @pl.when(jnp.logical_or(z == 0, jnp.logical_and(z == 1, k >= NA)))
-        def _():
-            wait(blk.at[0, k], blk_send.at[1, k])
-
-        @pl.when(jnp.logical_or(
-            z == 3,
-            jnp.logical_or(jnp.logical_and(z == 2, k < NA), jnp.logical_and(z == 0, k >= NA)),
-        ))
-        def _():
-            wait(blk.at[0, k], blk_send.at[2, k])
-
-        wait(sx.at[k], x_send.at[k])
-        wait(r1.at[k], s1_send.at[k])
-
-        @pl.when(k < NK - 1)
-        def _():
-            wait(r2.at[k], s2_send.at[k])
-            for ci in range(2):
-                @pl.when(core * 2 + ci != z)
-                def _():
-                    wait(s3.at[k, ci], z_send.at[k, ci])
-
-        @pl.when(mine)
-        def _():
-            wait(tf.at[k, 0:15], ag_send.at[k])
-            wait(ov.at[k, 0], o_send.at[k])
-
-        @pl.when(jnp.logical_not(mine))
-        def _():
-            wait(ov.at[k, 0], o_recv.at[k])
+        wait(ov.at[:, 0], o_recv)
 
 
 def local(
@@ -458,17 +453,17 @@
             vmem((NK, 48, W), B16),
             vmem((NK, 16, 48, W), B16),
             vmem((NK, 2, 24, W), F32),
-            dma((NK,)),
+            dma((2,)),
             dma((8,)),
-            dma((3, NK)),
+            dma((3,)),
             dma((4, NK)),
-            dma((NK,)), dma((NK,)),
-            dma((NK,)), dma((NK,)),
-            dma((NK,)), dma((NK,)),
-            dma((NK, 2)), dma((NK,)),
+            dma, dma((NK,)),
+            dma, dma((NK,)),
+            dma, dma((NK - 1,)),
+            dma, dma((NK - 1,)),
             dma, dma,
-            dma((NK,)), dma((NK,)),
-            dma((NK,)), dma((NK,)),
+            dma, dma((NK,)),
+            dma, dma,
         ],
         compiler_params=pltpu.CompilerParams(
             collective_id=0, has_side_effects=True, vmem_limit_bytes=52 * 1024 * 1024

time: 116 us -> 114 us (0.983)
    pallas_call x1, Pallas kernels: 111 us -> 110 us  [local(): pl.pallas_call(kernel, out_shape=(pltpu.VMEM((1, 1024, 1024), F32), pltpu...]
where the time goes in v4:
time: 114 us; the launch traced here: 113 us
  Pallas kernels  110 us (96%)
  local copies, waits for them, and re-layouts  2.66 us (2%)
    pallas_call x1, Pallas kernels, local(): pl.pallas_call(kernel, out_shape=(pltpu.VMEM((1, 1024, 1024), F32), pltpu...  110 us
    unnamed x2, local copies, waits for them, and re-layouts  2.66 us

profile of v4, /device:TPU:0, one launch (start us, length us, event | category | flops | bytes accessed | tf_op | source)
XLA Modules:
  0.0 113.1 jit_solution(10057226821781555967)
XLA Ops:
  0.6 109.8 %solve.1 = (f32[1,1024,1024]{2,1,0:T(8,128)S(1)}, f32[1,24,1024]{2,1,0:T(8,128)S(1)}) custom-call(s32[1,24]{1,0:T(1,128)} %flags.1, f32[1,1024,1024]{2,1,0:T(8,128)} %rhs_hbm.1, bf16[1,1024,4096]{2,1,0:T(8,128)(2,1)} %low_hbm.1, bf16[1,1024,1024]{2,1,0:T(8,128)(2,1)} %inv_hbm.1, bf16[1,3072,1024]{2,1,0:T(8,128)(2,1)} %cols_hbm.1, f32[768,1024]{1,0:T(8,128)} %side_hbm.1, ...), custom_call_target="tpu_custom_call" | custom-call | tf_op jit(solution)/shard_map/solve/pallas_call | solution.py:428
  110.4 2.0 %copy.11 = f32[1,1024,1024]{2,1,0:T(8,128)} copy(f32[1,1024,1024]{2,1,0:T(8,128)S(1)} %get-tuple-element.2) | data formatting | bytes 8388608
  112.4 0.6 copy.12

commit v5 on v4

--- a/solution.py
+++ b/solution.py
@@ -10,7 +10,9 @@
 NK = 8
 W = 128
 NA = 3
+NW = 6
 AHEAD = 5
+FAR = (2, 1, 3)
 B16 = jnp.bfloat16
 F32 = jnp.float32
 
@@ -198,7 +200,7 @@
                     total = own[slot, rows, :] + rx[k, rows, :].astype(F32)
                     at = ci * 192 + gg * 48
                     s1[k, ff, at:at + 48, :] = total.astype(B16)
-        for d in range(1, 4):
+        for d in FAR:
             to = lax.rem(f + d, 4)
             send(
                 s1.at[k, to], r1.at[k, d - 1], s1_send, s1_recv.at[k],
@@ -217,7 +219,7 @@
 
     def first_sum(k):
         first_total(k)
-        for d in range(1, 4):
+        for d in FAR:
             to = lax.rem(g + d, 4)
             send(
                 s2.at[k, to], r2.at[k, d - 1], s2_send, s2_recv.at[k],
@@ -227,14 +229,17 @@
     def wide_send(k):
         first_total(k)
         slot = z * 4 + g
-        for ci in range(2):
-            owner = core * 2 + ci
-            for d in range(4):
+        for d in FAR + (0,):
+            for ci in range(2):
+                owner = core * 2 + ci
                 to = lax.rem(g + d, 4)
                 piece = s2.at[k, to, ci * 48:(ci + 1) * 48, :]
 
                 def go():
-                    send(piece, rw.at[slot], w_send, w_recv, chip_of(f, to) * 2 + core, owner)
+                    send(
+                        piece, rw.at[k - NW, slot], w_send, w_recv.at[k - NW],
+                        chip_of(f, to) * 2 + core, owner,
+                    )
 
                 if d > 0:
                     go()
@@ -243,7 +248,7 @@
 
                     @pl.when(owner == z)
                     def _():
-                        rw[slot] = piece[...]
+                        rw[k - NW, slot] = piece[...]
 
     def second_sum(k):
         wait(r2.at[k], s2_recv.at[k])
@@ -266,10 +271,10 @@
     mine = lax.div(z, 2) == core
 
     def wide_sum(k):
-        wait(rw.at[0:15], w_recv)
-        total = rw[0].astype(F32)
+        wait(rw.at[k - NW, 0:15], w_recv.at[k - NW])
+        total = rw[k - NW, 0].astype(F32)
         for i in range(1, 16):
-            total += rw[i].astype(F32)
+            total += rw[k - NW, i].astype(F32)
         gather(k, total)
 
     def last_sum(k):
@@ -283,10 +288,11 @@
         here = sv[:, pl.ds(pl.multiple_of(k * W, W), W)]
         st[k] = (here - total).astype(B16)
 
-        @pl.loop(1, 16)
-        def _(i):
-            to = lax.rem(me + 2 * i, 32)
-            send(st.at[k], tf.at[k, chip], ag_send, ag_recv.at[k], to, z)
+        for d in FAR + (0,):
+            for e in FAR + (0,):
+                if d + e > 0:
+                    to = chip_of(lax.rem(f + d, 4), lax.rem(g + e, 4)) * 2 + core
+                    send(st.at[k], tf.at[k, chip], ag_send, ag_recv.at[k], to, z)
 
         tf[k, chip] = st[k]
 
@@ -358,23 +364,23 @@
             wait(blk.at[1, k], blk_recv.at[1, k])
             send_block(1, k, 2, 3)
 
-    first_sum(6)
+    wide_send(6)
     second_sum(4)
     second_sum(5)
     wide_send(7)
-    second_sum(6)
 
     @pl.when(jnp.logical_and(mine, z != 3))
     def _():
-        @pl.loop(0, NK - 1)
+        @pl.loop(0, NW)
         def _(k):
             last_sum(k)
 
     @pl.when(mine)
     def _():
+        wide_sum(6)
         wide_sum(7)
 
-    last_plane(last_sum, range(1, 7))
+    last_plane(last_sum, range(1, NW))
 
     @pl.when(z < 3)
     def _():
@@ -399,12 +405,12 @@
 
     wait(sx, x_send)
     wait(r1, s1_send)
-    wait(r2.at[0:NK - 1], s2_send)
+    wait(r2.at[0:NW], s2_send)
 
     @pl.when(mine)
     def _():
-        wait(s3.at[0:NK - 1, 0], z_send)
-        wait(rw.at[0:7], w_send)
+        wait(s3.at[0:NW, 0], z_send)
+        wait(rw.at[:, 0:7], w_send)
 
         @pl.loop(0, NK)
         def _(k):
@@ -415,8 +421,8 @@
 
     @pl.when(jnp.logical_not(mine))
     def _():
-        wait(s3.at[0:NK - 1], z_send)
-        wait(rw.at[0:8], w_send)
+        wait(s3.at[0:NW], z_send)
+        wait(rw.at[:, 0:8], w_send)
         wait(ov.at[:, 0], o_recv)
 
 
@@ -449,7 +455,7 @@
             vmem((NK, 3, 96, W), B16),
             vmem((NK, 2, 48, W), F32),
             vmem((NK, 3, 48, W), F32),
-            vmem((16, 48, W), B16),
+            vmem((NK - NW, 16, 48, W), B16),
             vmem((NK, 48, W), B16),
             vmem((NK, 16, 48, W), B16),
             vmem((NK, 2, 24, W), F32),
@@ -459,9 +465,9 @@
             dma((4, NK)),
             dma, dma((NK,)),
             dma, dma((NK,)),
-            dma, dma((NK - 1,)),
-            dma, dma((NK - 1,)),
-            dma, dma,
+            dma, dma((NW,)),
+            dma, dma((NW,)),
+            dma, dma((NK - NW,)),
             dma, dma((NK,)),
             dma, dma,
         ],

time: 114 us -> 114 us (level)
  no operation moved by 1% of the time
where the time goes in v5:
time: 114 us; the launch traced here: 112 us
  Pallas kernels  109 us (96%)
  local copies, waits for them, and re-layouts  2.66 us (2%)
    pallas_call x1, Pallas kernels, local(): pl.pallas_call(kernel, out_shape=(pltpu.VMEM((1, 1024, 1024), F32), pltpu...  109 us
    unnamed x2, local copies, waits for them, and re-layouts  2.66 us

profile of v5, /device:TPU:0, one launch (start us, length us, event | category | flops | bytes accessed | tf_op | source)
XLA Modules:
  0.0 112.4 jit_solution(4634216997313003602)
XLA Ops:
  0.6 109.1 %solve.1 = (f32[1,1024,1024]{2,1,0:T(8,128)S(1)}, f32[1,24,1024]{2,1,0:T(8,128)S(1)}) custom-call(s32[1,24]{1,0:T(1,128)} %flags.1, f32[1,1024,1024]{2,1,0:T(8,128)} %rhs_hbm.1, bf16[1,1024,4096]{2,1,0:T(8,128)(2,1)} %low_hbm.1, bf16[1,1024,1024]{2,1,0:T(8,128)(2,1)} %inv_hbm.1, bf16[1,3072,1024]{2,1,0:T(8,128)(2,1)} %cols_hbm.1, f32[768,1024]{1,0:T(8,128)} %side_hbm.1, ...), custom_call_target="tpu_custom_call" | custom-call | tf_op jit(solution)/shard_map/solve/pallas_call | solution.py:434
  109.8 2.0 %copy.11 = f32[1,1024,1024]{2,1,0:T(8,128)} copy(f32[1,1024,1024]{2,1,0:T(8,128)S(1)} %get-tuple-element.2) | data formatting | bytes 8388608
  111.8 0.6 copy.12
